TPU v7x, 32 devices: a whole 2x2x4 slice. The times are simulated.
32 devices in a mesh: ia: 4 (over y, core), ja: 2 (over x), ka: 4 (over z).
Axes of the slice: x: 2, y: 2, z: 4, core: 2. Of those that a mesh axis runs over, the one named last changes fastest.
Arguments:
- block_coords: int32 [4, 2, 4, 4, 3], P('ia', 'ja', 'ka'), may hold values from 0 to 3, as said below
- live_blocks: int32 [4, 2, 4], P('ia', 'ja', 'ka'), may hold values from 1 to 4, as said below
- counts: int32 [4, 2, 4, 4, 64, 4096], P('ia', 'ja', 'ka'), may hold values from 0 to 7
- factor_a: float32 [1024, 256], P(('ia', 'ja', 'ka')), may hold values from 0.3 to 9.6
- factor_b: float32 [512, 256], P(('ja', 'ka')), may hold values from 0.05 to 8
- factor_c: float32 [1024, 256], P('ka', 'ia'), may hold values from 0.05 to 8
Outputs:
- factor_new: float32 [1024, 256], P(('ia', 'ja', 'ka'))
Inputs may be any that keep to these rules, and one draw needn't show every extreme that they name: `block_coords`: a device's slots name distinct blocks; slot 0 is always live, and every mode-1 block of the slab has a live block on some device. `live_blocks`: on some device all 4 slots are live.
All inputs are finite; a program needn't handle non-finite values.
Results may differ from a plain program's by a relative error of at most 0.00061.
Values may be sent and summed in bfloat16 or wider, within the bound.
A program may use at most 64 MiB of HBM per device.

v0:
```python
import jax
import jax.numpy as jnp
from jax import lax
from jax.sharding import PartitionSpec as P

R = 256
BS = 64
RB1 = 4
RB2 = 4
RB3 = 4
SLOTS = 4


def make_panel(rows_b, rows_c, index_j, index_k):
    piece_b = lax.dynamic_slice_in_dim(rows_b, index_j * BS, BS, 0)
    piece_c = lax.dynamic_slice_in_dim(rows_c, index_k * BS, BS, 0)
    return (piece_b[:, None, :] * piece_c[None, :, :]).reshape(BS * BS, R).astype(jnp.bfloat16)


def add_block(phi, factor_low, panel, index_i, weight, block_counts):
    block_a = lax.dynamic_slice_in_dim(factor_low, index_i * BS, BS, 0)
    model = lax.dot_general(
        block_a, panel, (((1,), (1,)), ((), ())), preferred_element_type=jnp.float32
    )
    ratio = (block_counts.astype(jnp.float32) / model).astype(jnp.bfloat16)
    part = jnp.dot(ratio, panel, preferred_element_type=jnp.float32) * weight
    old = lax.dynamic_slice_in_dim(phi, index_i * BS, BS, 0)
    return lax.dynamic_update_slice_in_dim(phi, old + part, index_i * BS, 0)


def local(block_coords, live_blocks, counts, factor_a, factor_b, factor_c):
    coords = block_coords.reshape(SLOTS, 3)
    local_counts = counts.reshape(SLOTS, BS, BS * BS)
    weights = (jnp.arange(SLOTS, dtype=jnp.int32) < live_blocks.reshape(())).astype(jnp.float32)
    rows_b = lax.all_gather(factor_b, "ka", axis=0, tiled=True)
    rows_c = lax.all_gather(factor_c, "ia", axis=1, tiled=True)
    sums_b = rows_b.reshape(RB2, BS, R).sum(axis=1)
    sums_c = rows_c.reshape(RB3, BS, R).sum(axis=1)
    pick_j = (coords[:, 1:2] == jnp.arange(RB2, dtype=jnp.int32)[None, :]).astype(jnp.float32)
    pick_k = (coords[:, 2:3] == jnp.arange(RB3, dtype=jnp.int32)[None, :]).astype(jnp.float32)
    masses = jnp.dot(pick_j, sums_b, precision=lax.Precision.HIGHEST) * jnp.dot(
        pick_k, sums_c, precision=lax.Precision.HIGHEST
    )
    pick_i = (coords[:, 0:1] == jnp.arange(RB1, dtype=jnp.int32)[None, :]).astype(
        jnp.float32
    ) * weights[:, None]
    mass_part = lax.dot_general(
        pick_i, masses, (((0,), (0,)), ((), ())), precision=lax.Precision.HIGHEST
    )
    mass = lax.psum(mass_part, ("ja", "ka"))
    mass_rows = jnp.broadcast_to(mass[:, None, :], (RB1, BS, R)).reshape(RB1 * BS, R)
    owned = factor_a.shape[0]
    first_row = lax.axis_index(("ja", "ka")) * owned
    my_mass = lax.dynamic_slice_in_dim(mass_rows, first_row, owned, 0)
    empty = jnp.zeros((RB1 * BS, R), jnp.float32)

    def accumulate(factor_low):

        def step(phi, item):
            index_i, index_j, index_k, weight, block_counts = item
            panel = make_panel(rows_b, rows_c, index_j, index_k)
            return (add_block(phi, factor_low, panel, index_i, weight, block_counts), None)

        phi, _ = lax.scan(
            step, empty, (coords[:, 0], coords[:, 1], coords[:, 2], weights, local_counts)
        )
        return phi

    whole = lax.all_gather(factor_a, ("ja", "ka"), axis=0, tiled=True)
    phi = accumulate(whole.astype(jnp.bfloat16))
    totals = lax.psum(phi, ("ja", "ka"))
    updated = whole * totals / mass_rows
    phi = accumulate(updated.astype(jnp.bfloat16))
    mine = lax.psum_scatter(phi, ("ja", "ka"), scatter_dimension=0, tiled=True)
    return lax.dynamic_slice_in_dim(updated, first_row, owned, 0) * mine / my_mass


def solution(mesh):
    placed = (
        P("ia", "ja", "ka", None, None),
        P("ia", "ja", "ka"),
        P("ia", "ja", "ka", None, None, None),
        P(("ia", "ja", "ka"), None),
        P(("ja", "ka"), None),
        P("ka", "ia"),
    )
    return jax.shard_map(
        local, mesh=mesh, in_specs=placed, out_specs=P(("ia", "ja", "ka"), None), check_vma=False
    )
```

profile of v0, /device:TPU:0, one launch (start us, length us, event | category | flops | bytes accessed | tf_op | source)
XLA Modules:
  0.0 275.6 jit_solution(7233616077265290646)
XLA Ops:
  6.5 0.8 copy.14
  7.3 0.2 slice_reduce_fusion.2
  7.5 7.5 %all_gather.11 = f32[256,256]{0,1:T(8,128)S(1)} all-gather(f32[256,64]{0,1:T(8,128)} %param.15), channel_id=1, replica_groups=mesh['ia'=4,'ja'=2,'ka'=4] {'ia'}, dimensions={1}, use_global_device_ids=true | all-gather | bytes 327680 | tf_op jit(solution)/shard_map/all_gather | solution.py:36
  15.1 14.3 %all_gather.10 = f32[256,256]{1,0:T(8,128)S(1)} all-gather(f32[64,256]{1,0:T(8,128)} %param.14), channel_id=1, replica_groups=mesh['ia'=4,'ja'=2,'ka'=4] {'ka'}, dimensions={0}, use_global_device_ids=true | all-gather | bytes 327680 | tf_op jit(solution)/shard_map/all_gather | solution.py:35
  30.1 31.8 %all_gather.9 = f32[256,256]{1,0:T(8,128)S(1)} all-gather(f32[32,256]{1,0:T(8,128)} %param.13), channel_id=1, replica_groups=mesh['ia'=4,'ja'=2,'ka'=4] {'ja','ka'}, dimensions={0}, use_global_device_ids=true | all-gather | bytes 294912 | tf_op jit(solution)/shard_map/all_gather | solution.py:69
  62.0 34.4 %while.20 = (s32[]{:T(128)}, f32[256,256]{1,0:T(8,128)S(1)}, s32[4]{0:T(128)S(1)}, s32[4,64,4096]{2,1,0:T(8,128)}, bf16[256,256]{1,0:T(8,128)(2,1)S(1)}, /*index...) while((s32[]{:T(128)}, f32[256,256]{1,0:T(8,128)S(1)}, ...), condition=%wide.region_1.0_spmd, body=%wide.region_0.0_spmd.sunk | while | flops 271351808 | bytes 7899463 | solution.py:64
  62.0 0.7 dynamic_slice.108
  63.3 0.7 dynamic_slice.109
  64.7 0.7 multiply_convert_fusion.4
  65.4 0.7 dynamic_slice.107
  66.8 0.7 dynamic_slice.110
  67.5 3.1 %fusion.52 = f32[256,256]{1,0:T(8,128)S(1)} fusion(f32[256,256]{1,0:T(8,128)S(1)} %get-tuple-element.345, s32[]{:T(128)S(6)} %select_n.33, bf16[4096,256]{1,0:T(8,128)(2,1)S(1)} %bitcast.70, s32[4,64,4096]{2,1,0:T(8,128)} %get-tuple-element.361, s32[]{:T(128)} %get-tuple-element.344, f32[]{:T(128)} %bitcast.60, ...), kind=kOutput, calls=%fused_computation.6.clone.1 | convolution fusion | flops 269254656 | bytes 5408768 | tf_op jit(solution)/shard_map/while/body/eval_jaxpr/dot_general | solution.py:26
  70.6 0.7 dynamic_slice.108
  71.9 0.7 dynamic_slice.109
  73.3 0.7 multiply_convert_fusion.4
  74.0 0.7 dynamic_slice.107
  75.4 0.7 dynamic_slice.110
  76.1 3.1 %fusion.52 = f32[256,256]{1,0:T(8,128)S(1)} fusion(f32[256,256]{1,0:T(8,128)S(1)} %get-tuple-element.345, s32[]{:T(128)S(6)} %select_n.33, bf16[4096,256]{1,0:T(8,128)(2,1)S(1)} %bitcast.70, s32[4,64,4096]{2,1,0:T(8,128)} %get-tuple-element.361, s32[]{:T(128)} %get-tuple-element.344, f32[]{:T(128)} %bitcast.60, ...), kind=kOutput, calls=%fused_computation.6.clone.1 | convolution fusion | flops 269254656 | bytes 5408768 | tf_op jit(solution)/shard_map/while/body/eval_jaxpr/dot_general | solution.py:26
  79.2 0.7 dynamic_slice.108
  80.5 0.7 dynamic_slice.109
  81.9 0.7 multiply_convert_fusion.4
  82.6 0.7 dynamic_slice.107
  84.0 0.7 dynamic_slice.110
  84.7 3.1 %fusion.52 = f32[256,256]{1,0:T(8,128)S(1)} fusion(f32[256,256]{1,0:T(8,128)S(1)} %get-tuple-element.345, s32[]{:T(128)S(6)} %select_n.33, bf16[4096,256]{1,0:T(8,128)(2,1)S(1)} %bitcast.70, s32[4,64,4096]{2,1,0:T(8,128)} %get-tuple-element.361, s32[]{:T(128)} %get-tuple-element.344, f32[]{:T(128)} %bitcast.60, ...), kind=kOutput, calls=%fused_computation.6.clone.1 | convolution fusion | flops 269254656 | bytes 5408768 | tf_op jit(solution)/shard_map/while/body/eval_jaxpr/dot_general | solution.py:26
  87.8 0.7 dynamic_slice.108
  89.2 0.7 dynamic_slice.109
  90.5 0.7 multiply_convert_fusion.4
  91.2 0.7 dynamic_slice.107
  92.6 0.7 dynamic_slice.110
  93.3 3.1 %fusion.52 = f32[256,256]{1,0:T(8,128)S(1)} fusion(f32[256,256]{1,0:T(8,128)S(1)} %get-tuple-element.345, s32[]{:T(128)S(6)} %select_n.33, bf16[4096,256]{1,0:T(8,128)(2,1)S(1)} %bitcast.70, s32[4,64,4096]{2,1,0:T(8,128)} %get-tuple-element.361, s32[]{:T(128)} %get-tuple-element.344, f32[]{:T(128)} %bitcast.60, ...), kind=kOutput, calls=%fused_computation.6.clone.1 | convolution fusion | flops 269254656 | bytes 5408768 | tf_op jit(solution)/shard_map/while/body/eval_jaxpr/dot_general | solution.py:26
  96.4 0.7 copy-done.1
  97.4 0.2 convolution_multiply_fusion
  97.6 0.3 fusion.24
  97.9 21.7 %psum.15 = f32[4,256]{1,0:T(4,128)S(1)} all-reduce(f32[4,256]{1,0:T(4,128)S(1)} %fusion.24), channel_id=1, replica_groups=mesh['ia'=4,'ja'=2,'ka'=4] {'ja','ka'}, use_global_device_ids=true, to_apply=%region_5.6 | all-reduce | flops 1024 | bytes 8192 | tf_op jit(solution)/shard_map/psum | solution.py:50
  119.5 49.9 %all-reduce.2.cloned.1.call-done = f32[256,256]{1,0:T(8,128)} async-done(((f32[256,256]{1,0:T(8,128)}), f32[256,256]{1,0:T(8,128)}) %all-reduce.2.cloned.1.call-update) | async-done | bytes 262160 | tf_op jit(solution)/shard_map/psum | solution.py:71
  169.4 1.0 fusion.33
  170.5 34.4 %while.21 = (s32[]{:T(128)}, f32[256,256]{1,0:T(8,128)S(1)}, s32[4]{0:T(128)S(1)}, s32[4,64,4096]{2,1,0:T(8,128)}, bf16[256,256]{1,0:T(8,128)(2,1)S(1)}, /*index...) while((s32[]{:T(128)}, f32[256,256]{1,0:T(8,128)S(1)}, ...), condition=%wide.region_7.8_spmd, body=%wide.region_6.7_spmd.sunk | while | flops 271351808 | bytes 7899463 | solution.py:64
  170.5 0.7 dynamic_slice.116
  171.8 0.7 dynamic_slice.117
  173.2 0.7 multiply_convert_fusion.5
  173.9 0.7 dynamic_slice.115
  175.3 0.7 dynamic_slice.118
  176.0 3.1 %fusion.56 = f32[256,256]{1,0:T(8,128)S(1)} fusion(f32[256,256]{1,0:T(8,128)S(1)} %get-tuple-element.387, s32[]{:T(128)S(6)} %select_n.36, bf16[4096,256]{1,0:T(8,128)(2,1)S(1)} %bitcast.71, s32[4,64,4096]{2,1,0:T(8,128)} %get-tuple-element.403, s32[]{:T(128)} %get-tuple-element.386, f32[]{:T(128)} %bitcast.68, ...), kind=kOutput, calls=%fused_computation.20.clone.1 | convolution fusion | flops 269254656 | bytes 5408768 | tf_op jit(solution)/shard_map/while/body/eval_jaxpr/dot_general | solution.py:26
  179.1 0.7 dynamic_slice.116
  180.4 0.7 dynamic_slice.117
  181.8 0.7 multiply_convert_fusion.5
  182.5 0.7 dynamic_slice.115
  183.9 0.7 dynamic_slice.118
  184.6 3.1 %fusion.56 = f32[256,256]{1,0:T(8,128)S(1)} fusion(f32[256,256]{1,0:T(8,128)S(1)} %get-tuple-element.387, s32[]{:T(128)S(6)} %select_n.36, bf16[4096,256]{1,0:T(8,128)(2,1)S(1)} %bitcast.71, s32[4,64,4096]{2,1,0:T(8,128)} %get-tuple-element.403, s32[]{:T(128)} %get-tuple-element.386, f32[]{:T(128)} %bitcast.68, ...), kind=kOutput, calls=%fused_computation.20.clone.1 | convolution fusion | flops 269254656 | bytes 5408768 | tf_op jit(solution)/shard_map/while/body/eval_jaxpr/dot_general | solution.py:26
  187.7 0.7 dynamic_slice.116
  189.0 0.7 dynamic_slice.117
  190.4 0.7 multiply_convert_fusion.5
  191.1 0.7 dynamic_slice.115
  192.5 0.7 dynamic_slice.118
  193.2 3.1 %fusion.56 = f32[256,256]{1,0:T(8,128)S(1)} fusion(f32[256,256]{1,0:T(8,128)S(1)} %get-tuple-element.387, s32[]{:T(128)S(6)} %select_n.36, bf16[4096,256]{1,0:T(8,128)(2,1)S(1)} %bitcast.71, s32[4,64,4096]{2,1,0:T(8,128)} %get-tuple-element.403, s32[]{:T(128)} %get-tuple-element.386, f32[]{:T(128)} %bitcast.68, ...), kind=kOutput, calls=%fused_computation.20.clone.1 | convolution fusion | flops 269254656 | bytes 5408768 | tf_op jit(solution)/shard_map/while/body/eval_jaxpr/dot_general | solution.py:26
  196.3 0.7 dynamic_slice.116
  197.6 0.7 dynamic_slice.117
  199.0 0.7 multiply_convert_fusion.5
  199.7 0.7 dynamic_slice.115
  201.1 0.7 dynamic_slice.118
  201.8 3.1 %fusion.56 = f32[256,256]{1,0:T(8,128)S(1)} fusion(f32[256,256]{1,0:T(8,128)S(1)} %get-tuple-element.387, s32[]{:T(128)S(6)} %select_n.36, bf16[4096,256]{1,0:T(8,128)(2,1)S(1)} %bitcast.71, s32[4,64,4096]{2,1,0:T(8,128)} %get-tuple-element.403, s32[]{:T(128)} %get-tuple-element.386, f32[]{:T(128)} %bitcast.68, ...), kind=kOutput, calls=%fused_computation.20.clone.1 | convolution fusion | flops 269254656 | bytes 5408768 | tf_op jit(solution)/shard_map/while/body/eval_jaxpr/dot_general | solution.py:26
  204.9 0.7 copy-done
  205.6 61.8 %reduce-scatter.2.cloned.1.call-done = f32[32,256]{1,0:T(8,128)} async-done(((f32[256,256]{1,0:T(8,128)}), f32[32,256]{1,0:T(8,128)}) %reduce-scatter.2.cloned.1.call-update) | async-done | bytes 32784 | tf_op jit(solution)/shard_map/reduce_scatter | solution.py:74
  267.4 1.4 dynamic-slice_divide_fusion
  (23 shorter events, 0.7 us)
Async XLA Ops:
  6.5 162.9 %all-reduce.2.cloned.1.call-start = ((), (), s32[]{:S(2)}) async-start(), calls=%async_computation.1 | async-start | bytes 524288 | tf_op jit(solution)/shard_map/psum | solution.py:71
  96.4 0.7 copy-start.1
  97.1 170.3 %reduce-scatter.2.cloned.1.call-start = ((), (), s32[]{:S(2)}) async-start(), calls=%async_computation.2 | async-start | bytes 294912 | tf_op jit(solution)/shard_map/reduce_scatter | solution.py:74
  204.9 0.7 copy-start
Sparse Core Ops, SparseCore 0:
  97.2 72.1 all-reduce.1
  205.7 61.6 reduce-scatter.1
where the time goes:
time: 277 us; the launch traced here: 276 us
  waiting for transfers between devices  112 us (40%)
  blocking collectives  75.3 us (27%)
  matrix products  25.4 us (9%)
  local copies, waits for them, and re-layouts  24 us (9%)
  loops' own time  17.1 us (6%)
  between operations  14.1 us (5%)
  other arithmetic  7.95 us (3%)
    reduce_scatter x1, waiting for transfers between devices, local(): mine = lax.psum_scatter(phi, ('ja', 'ka'), scatter_dimension=0, tiled=True)  61.8 us
    psum x1, waiting for transfers between devices, local(): totals = lax.psum(phi, ('ja', 'ka'))  49.9 us
    all_gather x1, blocking collectives, local(): whole = lax.all_gather(factor_a, ('ja', 'ka'), axis=0, tiled=True)  31.8 us
    dot_general x8, matrix products, add_block(): part = jnp.dot(ratio, panel, preferred_element_type=jnp.float32) * weight  24.7 us
    psum x1, blocking collectives, local(): mass = lax.psum(mass_part, ('ja', 'ka'))  21.7 us
    dynamic_slice x32, local copies, waits for them, and re-layouts, accumulate(): lax.scan(step, empty, (coords[:, 0], coords[:, 1], coords[:, 2], weights,...  21.4 us
    another operation x2, loops' own time, accumulate(): lax.scan(step, empty, (coords[:, 0], coords[:, 1], coords[:, 2], weights,...  17.1 us
    all_gather x1, blocking collectives, local(): rows_b = lax.all_gather(factor_b, 'ka', axis=0, tiled=True)  14.3 us
  transfers between devices with their start and end apart: 2, of which 2 were waited for; matrix products, arithmetic and copies ran while one was open for 0% of the time, Pallas kernels for 0%

commit v1 on v0

--- a/solution.py
+++ b/solution.py
@@ -2,6 +2,7 @@
 import jax.numpy as jnp
 from jax import lax
 from jax.sharding import PartitionSpec as P
+from jax.lax import psum
 
 R = 256
 BS = 64
@@ -68,7 +69,8 @@
 
     whole = lax.all_gather(factor_a, ("ja", "ka"), axis=0, tiled=True)
     phi = accumulate(whole.astype(jnp.bfloat16))
-    totals = lax.psum(phi, ("ja", "ka"))
+    block_out = psum(phi, axis_name="ka")
+    totals = psum(block_out, axis_name="ja")
     updated = whole * totals / mass_rows
     phi = accumulate(updated.astype(jnp.bfloat16))
     mine = lax.psum_scatter(phi, ("ja", "ka"), scatter_dimension=0, tiled=True)

time: 277 us -> 267 us (0.964)
  waiting for transfers between devices: 112 us -> 104 us
    psum x1 -> x2, waiting for transfers between devices: 49.9 us -> 41.2 us  [the longest x1 36.5 us: local(): block_out = psum(phi, axis_name='ka')]
  transfers between devices with their start and end apart: 2 -> 3, of which waited for: 2 -> 3; matrix products, arithmetic and copies ran while one was open for 0% -> 0% of each run, Pallas kernels for 0% -> 0%
where the time goes in v1:
time: 267 us; the launch traced here: 266 us
  waiting for transfers between devices  104 us (39%)
  blocking collectives  74 us (28%)
  matrix products  25.4 us (10%)
  local copies, waits for them, and re-layouts  24 us (9%)
  loops' own time  17.1 us (6%)
  between operations  13.8 us (5%)
  other arithmetic  7.96 us (3%)
    reduce_scatter x1, waiting for transfers between devices, local(): mine = lax.psum_scatter(phi, ('ja', 'ka'), scatter_dimension=0, tiled=True)  62.6 us
    psum x1, waiting for transfers between devices, local(): block_out = psum(phi, axis_name='ka')  36.5 us
    all_gather x1, blocking collectives, local(): whole = lax.all_gather(factor_a, ('ja', 'ka'), axis=0, tiled=True)  31.8 us
    dot_general x8, matrix products, add_block(): part = jnp.dot(ratio, panel, preferred_element_type=jnp.float32) * weight  24.8 us
    dynamic_slice x32, local copies, waits for them, and re-layouts, accumulate(): lax.scan(step, empty, (coords[:, 0], coords[:, 1], coords[:, 2], weights,...  21.4 us
    psum x1, blocking collectives, local(): mass = lax.psum(mass_part, ('ja', 'ka'))  20.4 us
    another operation x2, loops' own time, accumulate(): lax.scan(step, empty, (coords[:, 0], coords[:, 1], coords[:, 2], weights,...  17.1 us
    all_gather x1, blocking collectives, local(): rows_b = lax.all_gather(factor_b, 'ka', axis=0, tiled=True)  14.3 us
  transfers between devices with their start and end apart: 3, of which 3 were waited for; matrix products, arithmetic and copies ran while one was open for 0% of the time, Pallas kernels for 0%

profile of v1, /device:TPU:0, one launch (start us, length us, event | category | flops | bytes accessed | tf_op | source)
XLA Modules:
  0.0 266.3 jit_solution(2903980217069420917)
XLA Ops:
  6.5 0.8 copy.14
  7.3 0.2 slice_reduce_fusion.2
  7.5 7.5 %all_gather.11 = f32[256,256]{0,1:T(8,128)S(1)} all-gather(f32[256,64]{0,1:T(8,128)} %param.15), channel_id=1, replica_groups=mesh['ia'=4,'ja'=2,'ka'=4] {'ia'}, dimensions={1}, use_global_device_ids=true | all-gather | bytes 327680 | tf_op jit(solution)/shard_map/all_gather | solution.py:37
  15.1 14.3 %all_gather.10 = f32[256,256]{1,0:T(8,128)S(1)} all-gather(f32[64,256]{1,0:T(8,128)} %param.14), channel_id=1, replica_groups=mesh['ia'=4,'ja'=2,'ka'=4] {'ka'}, dimensions={0}, use_global_device_ids=true | all-gather | bytes 327680 | tf_op jit(solution)/shard_map/all_gather | solution.py:36
  30.1 31.8 %all_gather.9 = f32[256,256]{1,0:T(8,128)S(1)} all-gather(f32[32,256]{1,0:T(8,128)} %param.13), channel_id=1, replica_groups=mesh['ia'=4,'ja'=2,'ka'=4] {'ja','ka'}, dimensions={0}, use_global_device_ids=true | all-gather | bytes 294912 | tf_op jit(solution)/shard_map/all_gather | solution.py:70
  62.0 34.5 %while.20 = (s32[]{:T(128)}, f32[256,256]{1,0:T(8,128)S(1)}, s32[4]{0:T(128)S(1)}, s32[4,64,4096]{2,1,0:T(8,128)}, bf16[256,256]{1,0:T(8,128)(2,1)S(1)}, /*index...) while((s32[]{:T(128)}, f32[256,256]{1,0:T(8,128)S(1)}, ...), condition=%wide.region_1.0_spmd, body=%wide.region_0.0_spmd.sunk | while | flops 271351808 | bytes 7899463 | solution.py:65
  62.0 0.7 dynamic_slice.108
  63.3 0.7 dynamic_slice.109
  64.7 0.7 multiply_convert_fusion.4
  65.4 0.7 dynamic_slice.107
  66.8 0.7 dynamic_slice.110
  67.5 3.1 %fusion.52 = f32[256,256]{1,0:T(8,128)S(1)} fusion(f32[256,256]{1,0:T(8,128)S(1)} %get-tuple-element.345, s32[]{:T(128)S(6)} %select_n.33, bf16[4096,256]{1,0:T(8,128)(2,1)S(1)} %bitcast.70, s32[4,64,4096]{2,1,0:T(8,128)} %get-tuple-element.361, s32[]{:T(128)} %get-tuple-element.344, f32[]{:T(128)} %bitcast.60, ...), kind=kOutput, calls=%fused_computation.6.clone.1 | convolution fusion | flops 269254656 | bytes 5408768 | tf_op jit(solution)/shard_map/while/body/eval_jaxpr/dot_general | solution.py:27
  70.6 0.7 dynamic_slice.108
  71.9 0.7 dynamic_slice.109
  73.3 0.7 multiply_convert_fusion.4
  74.0 0.7 dynamic_slice.107
  75.4 0.7 dynamic_slice.110
  76.1 3.1 %fusion.52 = f32[256,256]{1,0:T(8,128)S(1)} fusion(f32[256,256]{1,0:T(8,128)S(1)} %get-tuple-element.345, s32[]{:T(128)S(6)} %select_n.33, bf16[4096,256]{1,0:T(8,128)(2,1)S(1)} %bitcast.70, s32[4,64,4096]{2,1,0:T(8,128)} %get-tuple-element.361, s32[]{:T(128)} %get-tuple-element.344, f32[]{:T(128)} %bitcast.60, ...), kind=kOutput, calls=%fused_computation.6.clone.1 | convolution fusion | flops 269254656 | bytes 5408768 | tf_op jit(solution)/shard_map/while/body/eval_jaxpr/dot_general | solution.py:27
  79.2 0.7 dynamic_slice.108
  80.6 0.7 dynamic_slice.109
  82.0 0.7 multiply_convert_fusion.4
  82.6 0.7 dynamic_slice.107
  84.0 0.7 dynamic_slice.110
  84.7 3.1 %fusion.52 = f32[256,256]{1,0:T(8,128)S(1)} fusion(f32[256,256]{1,0:T(8,128)S(1)} %get-tuple-element.345, s32[]{:T(128)S(6)} %select_n.33, bf16[4096,256]{1,0:T(8,128)(2,1)S(1)} %bitcast.70, s32[4,64,4096]{2,1,0:T(8,128)} %get-tuple-element.361, s32[]{:T(128)} %get-tuple-element.344, f32[]{:T(128)} %bitcast.60, ...), kind=kOutput, calls=%fused_computation.6.clone.1 | convolution fusion | flops 269254656 | bytes 5408768 | tf_op jit(solution)/shard_map/while/body/eval_jaxpr/dot_general | solution.py:27
  87.8 0.7 dynamic_slice.108
  89.2 0.7 dynamic_slice.109
  90.6 0.7 multiply_convert_fusion.4
  91.3 0.7 dynamic_slice.107
  92.6 0.7 dynamic_slice.110
  93.3 3.1 %fusion.52 = f32[256,256]{1,0:T(8,128)S(1)} fusion(f32[256,256]{1,0:T(8,128)S(1)} %get-tuple-element.345, s32[]{:T(128)S(6)} %select_n.33, bf16[4096,256]{1,0:T(8,128)(2,1)S(1)} %bitcast.70, s32[4,64,4096]{2,1,0:T(8,128)} %get-tuple-element.361, s32[]{:T(128)} %get-tuple-element.344, f32[]{:T(128)} %bitcast.60, ...), kind=kOutput, calls=%fused_computation.6.clone.1 | convolution fusion | flops 269254656 | bytes 5408768 | tf_op jit(solution)/shard_map/while/body/eval_jaxpr/dot_general | solution.py:27
  96.4 0.7 copy-done.1
  97.4 36.5 %all-reduce.3.cloned.1.call-done = f32[256,256]{1,0:T(8,128)} async-done(((f32[256,256]{1,0:T(8,128)}), f32[256,256]{1,0:T(8,128)}) %all-reduce.3.cloned.1.call-update) | async-done | bytes 262160 | tf_op jit(solution)/shard_map/psum | solution.py:72
  134.2 0.3 fusion.24
  134.5 20.4 %psum.23 = f32[4,256]{1,0:T(4,128)S(1)} all-reduce(f32[4,256]{1,0:T(4,128)S(1)} %fusion.24), channel_id=1, replica_groups=mesh['ia'=4,'ja'=2,'ka'=4] {'ja','ka'}, use_global_device_ids=true, to_apply=%region_6.7 | all-reduce | flops 1024 | bytes 8192 | tf_op jit(solution)/shard_map/psum | solution.py:51
  154.9 4.6 %all-reduce.5.cloned.1.call-done = f32[256,256]{1,0:T(8,128)} async-done(((f32[256,256]{1,0:T(8,128)}), f32[256,256]{1,0:T(8,128)}) %all-reduce.5.cloned.1.call-update) | async-done | bytes 262160 | tf_op jit(solution)/shard_map/psum | solution.py:73
  159.5 1.0 fusion.33
  160.6 34.4 %while.21 = (s32[]{:T(128)}, f32[256,256]{1,0:T(8,128)S(1)}, s32[4]{0:T(128)S(1)}, s32[4,64,4096]{2,1,0:T(8,128)}, bf16[256,256]{1,0:T(8,128)(2,1)S(1)}, /*index...) while((s32[]{:T(128)}, f32[256,256]{1,0:T(8,128)S(1)}, ...), condition=%wide.region_8.9_spmd, body=%wide.region_7.8_spmd.sunk | while | flops 271351808 | bytes 7899463 | solution.py:65
  160.6 0.7 dynamic_slice.116
  161.9 0.7 dynamic_slice.117
  163.3 0.7 multiply_convert_fusion.5
  164.0 0.7 dynamic_slice.115
  165.4 0.7 dynamic_slice.118
  166.1 3.1 %fusion.56 = f32[256,256]{1,0:T(8,128)S(1)} fusion(f32[256,256]{1,0:T(8,128)S(1)} %get-tuple-element.387, s32[]{:T(128)S(6)} %select_n.36, bf16[4096,256]{1,0:T(8,128)(2,1)S(1)} %bitcast.71, s32[4,64,4096]{2,1,0:T(8,128)} %get-tuple-element.403, s32[]{:T(128)} %get-tuple-element.386, f32[]{:T(128)} %bitcast.68, ...), kind=kOutput, calls=%fused_computation.20.clone.1 | convolution fusion | flops 269254656 | bytes 5408768 | tf_op jit(solution)/shard_map/while/body/eval_jaxpr/dot_general | solution.py:27
  169.2 0.7 dynamic_slice.116
  170.6 0.7 dynamic_slice.117
  172.0 0.7 multiply_convert_fusion.5
  172.6 0.7 dynamic_slice.115
  174.0 0.7 dynamic_slice.118
  174.7 3.1 %fusion.56 = f32[256,256]{1,0:T(8,128)S(1)} fusion(f32[256,256]{1,0:T(8,128)S(1)} %get-tuple-element.387, s32[]{:T(128)S(6)} %select_n.36, bf16[4096,256]{1,0:T(8,128)(2,1)S(1)} %bitcast.71, s32[4,64,4096]{2,1,0:T(8,128)} %get-tuple-element.403, s32[]{:T(128)} %get-tuple-element.386, f32[]{:T(128)} %bitcast.68, ...), kind=kOutput, calls=%fused_computation.20.clone.1 | convolution fusion | flops 269254656 | bytes 5408768 | tf_op jit(solution)/shard_map/while/body/eval_jaxpr/dot_general | solution.py:27
  177.8 0.7 dynamic_slice.116
  179.2 0.7 dynamic_slice.117
  180.6 0.7 multiply_convert_fusion.5
  181.3 0.7 dynamic_slice.115
  182.6 0.7 dynamic_slice.118
  183.3 3.1 %fusion.56 = f32[256,256]{1,0:T(8,128)S(1)} fusion(f32[256,256]{1,0:T(8,128)S(1)} %get-tuple-element.387, s32[]{:T(128)S(6)} %select_n.36, bf16[4096,256]{1,0:T(8,128)(2,1)S(1)} %bitcast.71, s32[4,64,4096]{2,1,0:T(8,128)} %get-tuple-element.403, s32[]{:T(128)} %get-tuple-element.386, f32[]{:T(128)} %bitcast.68, ...), kind=kOutput, calls=%fused_computation.20.clone.1 | convolution fusion | flops 269254656 | bytes 5408768 | tf_op jit(solution)/shard_map/while/body/eval_jaxpr/dot_general | solution.py:27
  186.4 0.7 dynamic_slice.116
  187.8 0.7 dynamic_slice.117
  189.2 0.7 multiply_convert_fusion.5
  189.9 0.7 dynamic_slice.115
  191.2 0.7 dynamic_slice.118
  191.9 3.1 %fusion.56 = f32[256,256]{1,0:T(8,128)S(1)} fusion(f32[256,256]{1,0:T(8,128)S(1)} %get-tuple-element.387, s32[]{:T(128)S(6)} %select_n.36, bf16[4096,256]{1,0:T(8,128)(2,1)S(1)} %bitcast.71, s32[4,64,4096]{2,1,0:T(8,128)} %get-tuple-element.403, s32[]{:T(128)} %get-tuple-element.386, f32[]{:T(128)} %bitcast.68, ...), kind=kOutput, calls=%fused_computation.20.clone.1 | convolution fusion | flops 269254656 | bytes 5408768 | tf_op jit(solution)/shard_map/while/body/eval_jaxpr/dot_general | solution.py:27
  195.0 0.7 copy-done
  195.7 62.6 %reduce-scatter.2.cloned.1.call-done = f32[32,256]{1,0:T(8,128)} async-done(((f32[256,256]{1,0:T(8,128)}), f32[32,256]{1,0:T(8,128)}) %reduce-scatter.2.cloned.1.call-update) | async-done | bytes 32784 | tf_op jit(solution)/shard_map/reduce_scatter | solution.py:76
  258.3 1.4 dynamic-slice_divide_fusion
  (26 shorter events, 0.9 us)
Async XLA Ops:
  6.5 127.4 %all-reduce.3.cloned.1.call-start = ((), (), s32[]{:S(2)}) async-start(), calls=%async_computation.1 | async-start | bytes 524288 | tf_op jit(solution)/shard_map/psum | solution.py:72
  96.4 0.7 copy-start.1
  97.1 62.4 %all-reduce.5.cloned.1.call-start = ((), (), s32[]{:S(2)}) async-start(), calls=%async_computation.2 | async-start | bytes 524288 | tf_op jit(solution)/shard_map/psum | solution.py:73
  134.0 124.3 %reduce-scatter.2.cloned.1.call-start = ((), (), s32[]{:S(2)}) async-start(), calls=%async_computation.3 | async-start | bytes 294912 | tf_op jit(solution)/shard_map/reduce_scatter | solution.py:76
  195.0 0.7 copy-start
Sparse Core Ops, SparseCore 0:
  97.3 36.6 all-reduce.2
  136.2 23.2 all-reduce.4
  195.8 62.4 reduce-scatter.1
